TPU v7x, 32 devices: a whole 2x2x4 slice. The times are simulated.
32 devices in a mesh: dir: 2 (over x), sx: 4 (over y, core), sy: 4 (over z).
Axes of the slice: x: 2, y: 2, z: 4, core: 2. Of those that a mesh axis runs over, the one named last changes fastest.
Arguments:
- signs_x: int32 [2, 256], P('dir', 'sx'), may hold values from -2147483648 to 2147483647, as said below
- signs_y: int32 [2, 512], P('dir', 'sy'), may hold values from -2147483648 to 2147483647, as said below
- heights: int32 [256, 512], P('sx', 'sy'), may hold values from 0 to 63
- velocity: float32 [256, 512], P('sx', 'sy'), may hold values from 1 to 2
- background: float32 [2, 256, 512], P('dir', 'sx', 'sy'), may hold values from -4 to 4
Outputs:
- basis: float32 [64, 256, 512], P('dir', 'sx', 'sy')
- factor: float32 [64, 64], P('dir')
Inputs may be any that keep to these rules, and one draw needn't show every extreme that they name: `signs_x`: packed sign words, every bit pattern possible. `signs_y`: packed sign words, every bit pattern possible.
All inputs are finite; a program needn't handle non-finite values.
Results may differ from a plain program's by a relative error of at most 0.00027.
Values sent between devices are 32-bit elements; how exact they have to be, the bound alone decides.
A program may use at most 64 MiB of HBM per device.

v0:
```python
import math
import jax
import jax.numpy as jnp
from jax import lax
from jax.sharding import PartitionSpec as P

PROBES = 32
LEVELS = 64
tau_step = 0.02


def with_halo(cells, sides, width):
    for axis, dim in sides:
        count = lax.axis_size(axis)
        ends = count - 1
        head = lax.slice_in_dim(cells, 0, width, axis=dim)
        tail = lax.slice_in_dim(cells, cells.shape[dim] - width, cells.shape[dim], axis=dim)
        cells = jnp.concatenate(
            [
                lax.ppermute(tail, axis, [(i, (i + 1) % count) for i in range(ends)]),
                cells,
                lax.ppermute(head, axis, [((i + 1) % count, i) for i in range(ends)]),
            ],
            axis=dim,
        )
    return cells


def unpack_signs(packed, per_group):
    bit_index = jnp.arange(per_group, dtype=jnp.int32)
    bit_values = jnp.right_shift(packed[:, None, :], bit_index[None, :, None]) & 1
    signed = (2 * bit_values - 1).astype(jnp.float32)
    return signed.reshape(packed.shape[0] * per_group, packed.shape[1])


def apply_step(wavefield, stiffness):
    weighted = stiffness * wavefield
    padded = with_halo(weighted, (("sx", 1), ("sy", 2)), 1)
    laplace = (
        padded[:, 2:, 1:-1]
        + padded[:, :-2, 1:-1]
        + padded[:, 1:-1, 2:]
        + padded[:, 1:-1, :-2]
        - 4.0 * weighted
    )
    return wavefield + tau_step * stiffness * laplace


def responses_for(signs_first, signs_second, shot_data, stiffness):
    first_signs = unpack_signs(signs_first, PROBES)
    second = unpack_signs(signs_second, PROBES)
    kronecker = first_signs[:, :, None] * second[:, None, :]
    groups = shot_data.shape[0]
    rows_x = shot_data.shape[1]
    rows_y = shot_data.shape[2]
    rolled = jnp.roll(kronecker.reshape(groups, PROBES, rows_x, rows_y), -1, axis=1).reshape(
        kronecker.shape
    )
    probe_dirs = kronecker + 0.5 * rolled
    shot_fields = jnp.repeat(shot_data, PROBES, axis=0)
    wavefield = shot_fields * probe_dirs
    for repeat in range(4):
        wavefield = apply_step(wavefield, stiffness[None])
    return (shot_fields * wavefield).reshape(groups * PROBES, rows_x * rows_y)


def shards(signs_x, signs_y, heights, velocity, background):
    rows_x = background.shape[1]
    rows_y = background.shape[2]
    stiffness = velocity * jnp.sqrt(1.0 + heights.astype(jnp.float32) / LEVELS)
    response = responses_for(signs_x, signs_y, background, stiffness)
    all_rows = lax.all_gather(response, "dir", axis=0, tiled=True)
    local_gram = jnp.dot(
        all_rows, all_rows.T, precision=lax.Precision.HIGHEST, preferred_element_type=jnp.float32
    )
    gram_matrix = lax.psum(local_gram, ("sx", "sy"))
    factor_low = jnp.linalg.cholesky(gram_matrix)
    orthonormal = lax.linalg.triangular_solve(factor_low, all_rows, left_side=True, lower=True)
    factor_r = factor_low.T
    cell_count = math.sqrt(rows_x * rows_y * lax.axis_size("sx") * lax.axis_size("sy"))
    row_start = lax.axis_index("dir") * PROBES
    own_q = lax.dynamic_slice_in_dim(orthonormal, row_start, PROBES, 0)
    own_r = lax.dynamic_slice_in_dim(factor_r, row_start, PROBES, 0)
    basis = (own_q * cell_count).reshape(PROBES, rows_x, rows_y)
    factor = own_r / cell_count
    return (basis, factor)


def solution(mesh):
    in_specs = (P("dir", "sx"), P("dir", "sy"), P("sx", "sy"), P("sx", "sy"), P("dir", "sx", "sy"))
    out_specs = (P("dir", "sx", "sy"), P("dir", None))
    return jax.shard_map(shards, mesh=mesh, in_specs=in_specs, out_specs=out_specs, check_vma=False)
```

profile of v0, /device:TPU:0, one launch (start us, length us, event | category | flops | bytes accessed | tf_op | source)
XLA Modules:
  0.0 231.4 jit_solution(7985730447501686642)
XLA Ops:
  7.2 0.7 add_convert_fusion
  7.9 0.7 add_convert_fusion.1
  8.6 0.3 broadcast_multiply_fusion.3
  9.0 0.1 slice.164
  9.2 0.5 copy-done.3
  9.8 0.4 fusion.29
  10.2 1.3 collective-permute-start
  11.5 3.0 %collective-permute-start.1 = (f32[32,1,128]{2,0,1:T(8,128)S(1)}, f32[32,1,128]{2,0,1:T(8,128)S(1)}, u32[]{:S(2)}, u32[]{:S(2)}) collective-permute-start(f32[32,1,128]{2,0,1:T(8,128)S(1)} %get-tuple-element.34), channel_id=1, source_target_pairs={{0,4},{4,8},{8,12},{1,5},{5,9},{9,13},{2,6},{6,10},{10,14},{3,7},{... | collective-permute-start | bytes 49160 | tf_op jit(solution)/shard_map/ppermute | solution.py:20
  14.5 0.8 collective-permute-done.1
  15.4 1.8 fusion.39
  17.1 1.9 copy.23
  19.0 1.3 collective-permute-start.2
  20.3 1.9 copy.25
  22.2 5.6 %collective-permute-start.3 = (f32[32,66,1]{1,0,2:T(8,128)S(1)}, f32[32,66,1]{1,0,2:T(8,128)S(1)}, u32[]{:S(2)}, u32[]{:S(2)}) collective-permute-start(f32[32,66,1]{1,0,2:T(8,128)S(1)} %copy.25), channel_id=1, source_target_pairs={{0,1},{1,2},{2,3},{4,5},{5,6},{6,7},{8,9},{9,10},{10,11},{12,13},{... | collective-permute-start | bytes 25352 | tf_op jit(solution)/shard_map/ppermute | solution.py:20
  27.7 1.9 copy.24
  29.6 1.9 copy.26
  31.6 3.9 %broadcast_multiply_fusion.2 = (f32[32,64,128]{2,0,1:T(8,128)S(1)}, f32[32,64,128]{2,0,1:T(8,128)}) fusion(f32[64,128]{1,0:T(8,128)S(1)} %get-tuple-element.19, f32[32,64,128]{2,0,1:T(8,128)S(1)} %fusion.29, f32[32,1,128]{2,0,1:T(8,128)S(1)} %collective-permute-done, f32[32,1,128]{2,0,1:T(8,128)S(1)} %collective-permute-done.1, f32[32,66,1]{2,0,1:T(8,128)} %copy.26, ...), kind=kLoop, calls=%fused_computation.71 | loop fusion | flops 5505024 | bytes 4366848 | tf_op jit(solution)/shard_map/mul | solution.py:37
  35.5 1.3 collective-permute-start.4
  36.8 3.6 %collective-permute-start.5 = (f32[32,1,128]{2,0,1:T(8,128)S(1)}, f32[32,1,128]{2,0,1:T(8,128)S(1)}, u32[]{:S(2)}, u32[]{:S(2)}) collective-permute-start(f32[32,1,128]{2,0,1:T(8,128)S(1)} %get-tuple-element.32), channel_id=1, source_target_pairs={{0,4},{4,8},{8,12},{1,5},{5,9},{9,13},{2,6},{6,10},{10,14},{3,7},{... | collective-permute-start | bytes 49160 | tf_op jit(solution)/shard_map/ppermute | solution.py:20
  40.3 0.8 collective-permute-done.5
  41.2 1.4 fusion.38
  42.6 1.9 copy.27
  44.5 1.3 collective-permute-start.6
  45.8 0.7 copy.29
  46.5 4.5 %collective-permute-start.7 = (f32[32,66,1]{1,0,2:T(8,128)S(1)}, f32[32,66,1]{1,0,2:T(8,128)S(1)}, u32[]{:S(2)}, u32[]{:S(2)}) collective-permute-start(f32[32,66,1]{1,0,2:T(8,128)S(1)} %copy.29), channel_id=1, source_target_pairs={{0,1},{1,2},{2,3},{4,5},{5,6},{6,7},{8,9},{9,10},{10,11},{12,13},{... | collective-permute-start | bytes 25352 | tf_op jit(solution)/shard_map/ppermute | solution.py:20
  51.0 1.1 copy.28
  52.1 0.3 collective-permute-done.7
  52.5 1.9 copy.30
  54.4 3.4 %broadcast_multiply_fusion.1 = (f32[32,64,128]{2,0,1:T(8,128)S(1)}, f32[32,64,128]{2,0,1:T(8,128)}) fusion(f32[64,128]{1,0:T(8,128)S(1)} %get-tuple-element.19, f32[32,64,128]{2,0,1:T(8,128)} %get-tuple-element.17, f32[32,64,128]{2,0,1:T(8,128)S(1)} %get-tuple-element.16, f32[32,1,128]{2,0,1:T(8,128)S(1)} %collective-permute-done.4, ...), kind=kLoop, calls=%fused_computation.70 | loop fusion | flops 4194304 | bytes 4309504 | tf_op jit(solution)/shard_map/mul | solution.py:37
  57.8 1.3 collective-permute-start.8
  59.1 4.6 %collective-permute-start.9 = (f32[32,1,128]{2,0,1:T(8,128)S(1)}, f32[32,1,128]{2,0,1:T(8,128)S(1)}, u32[]{:S(2)}, u32[]{:S(2)}) collective-permute-start(f32[32,1,128]{2,0,1:T(8,128)S(1)} %get-tuple-element.30), channel_id=1, source_target_pairs={{0,4},{4,8},{8,12},{1,5},{5,9},{9,13},{2,6},{6,10},{10,14},{3,7},{... | collective-permute-start | bytes 49160 | tf_op jit(solution)/shard_map/ppermute | solution.py:20
  63.7 0.8 collective-permute-done.9
  64.6 0.4 fusion.37
  64.9 0.7 copy.31
  65.7 1.3 collective-permute-start.10
  67.0 0.7 copy.33
  67.7 4.7 %collective-permute-start.11 = (f32[32,66,1]{1,0,2:T(8,128)S(1)}, f32[32,66,1]{1,0,2:T(8,128)S(1)}, u32[]{:S(2)}, u32[]{:S(2)}) collective-permute-start(f32[32,66,1]{1,0,2:T(8,128)S(1)} %copy.33), channel_id=1, source_target_pairs={{0,1},{1,2},{2,3},{4,5},{5,6},{6,7},{8,9},{9,10},{10,11},{12,13},{... | collective-permute-start | bytes 25352 | tf_op jit(solution)/shard_map/ppermute | solution.py:20
  72.4 1.1 copy.32
  73.5 0.2 collective-permute-done.11
  73.7 1.9 copy.34
  75.6 3.4 %broadcast_multiply_fusion = (f32[32,64,128]{2,0,1:T(8,128)S(1)}, f32[32,64,128]{2,0,1:T(8,128)}) fusion(f32[64,128]{1,0:T(8,128)S(1)} %get-tuple-element.19, f32[32,64,128]{2,0,1:T(8,128)} %get-tuple-element.15, f32[32,64,128]{2,0,1:T(8,128)S(1)} %get-tuple-element.14, f32[32,1,128]{2,0,1:T(8,128)S(1)} %collective-permute-done.8, ...), kind=kLoop, calls=%fused_computation.69 | loop fusion | flops 4194304 | bytes 4309504 | tf_op jit(solution)/shard_map/mul | solution.py:37
  79.0 1.3 collective-permute-start.12
  80.3 5.5 %collective-permute-start.13 = (f32[32,1,128]{2,0,1:T(8,128)S(1)}, f32[32,1,128]{2,0,1:T(8,128)S(1)}, u32[]{:S(2)}, u32[]{:S(2)}) collective-permute-start(f32[32,1,128]{2,0,1:T(8,128)S(1)} %get-tuple-element.28), channel_id=1, source_target_pairs={{0,4},{4,8},{8,12},{1,5},{5,9},{9,13},{2,6},{6,10},{10,14},{3,7},{... | collective-permute-start | bytes 49160 | tf_op jit(solution)/shard_map/ppermute | solution.py:20
  85.8 0.8 collective-permute-done.13
  86.7 1.4 fusion.36
  88.1 1.9 copy.35
  89.9 1.3 collective-permute-start.14
  91.2 0.7 copy.37
  91.9 4.7 %collective-permute-start.15 = (f32[32,66,1]{1,0,2:T(8,128)S(1)}, f32[32,66,1]{1,0,2:T(8,128)S(1)}, u32[]{:S(2)}, u32[]{:S(2)}) collective-permute-start(f32[32,66,1]{1,0,2:T(8,128)S(1)} %copy.37), channel_id=1, source_target_pairs={{0,1},{1,2},{2,3},{4,5},{5,6},{6,7},{8,9},{9,10},{10,11},{12,13},{... | collective-permute-start | bytes 25352 | tf_op jit(solution)/shard_map/ppermute | solution.py:20
  96.6 1.1 copy.36
  97.7 0.3 collective-permute-done.15
  98.1 1.9 copy.38
  100.0 3.1 %copy_bitcast_fusion = f32[32,8192]{1,0:T(8,128)} fusion(f32[32,64,128]{2,0,1:T(8,128)S(1)} %copy-done.1, f32[32,66,1]{2,0,1:T(8,128)} %copy.38, f32[32,1,128]{2,0,1:T(8,128)S(1)} %collective-permute-done.12, f32[32,64,128]{2,0,1:T(8,128)S(1)} %get-tuple-element.12, f32[32,1,128]{2,0,1:T(8,128)S(1)} %collective-permute-done.13, f32[32,66,1]{2,0,1:T(8,128)S(1)} %copy.36, ...), kind=kLoop, calls=%fused_computation.4 | loop fusion | flops 4194304 | bytes 3260928 | tf_op jit(solution)/shard_map/reshape | solution.py:64
  103.1 39.8 %all-gather.2.cloned.1.call-done = f32[64,8192]{1,0:T(8,128)} async-done(((f32[32,8192]{1,0:T(8,128)}), f32[64,8192]{1,0:T(8,128)}) %all-gather.2.cloned.1.call-update) | async-done | bytes 2097168 | tf_op jit(solution)/shard_map/all_gather | solution.py:72
  142.9 4.2 %fusion.44 = f32[64,64]{0,1:T(8,128)S(1)} fusion(f32[64,8192]{1,0:T(8,128)} %all-gather.2.cloned.1.call-done), kind=kOutput, calls=%fused_computation.96 | convolution fusion | flops 402653184 | bytes 2113536 | tf_op jit(solution)/shard_map/dot_general | solution.py:73
  147.1 61.3 %psum.7 = f32[64,64]{0,1:T(8,128)S(1)} all-reduce(f32[64,64]{0,1:T(8,128)S(1)} %fusion.44), channel_id=1, replica_groups=mesh['dir'=2,'sx'=4,'sy'=4] {'sx','sy'}, use_global_device_ids=true, to_apply=%region_0.1 | all-reduce | flops 4096 | bytes 32768 | tf_op jit(solution)/shard_map/psum | solution.py:76
  208.5 5.8 %cholesky.16 = f32[64,64]{1,0:T(8,128)S(1)} custom-call(f32[64,64]{1,0:T(8,128)S(1)} %fusion.32), custom_call_target="Cholesky" | custom-call | tf_op jit(solution)/shard_map/jit(cholesky)/cholesky | solution.py:77
  214.3 0.6 compare_reduce_fusion
  215.0 0.7 select_bitcast_fusion
  215.7 4.9 %custom-call.6 = f32[1,64,64]{1,2,0:T(8,128)S(1)} custom-call(f32[1,64,64]{2,1,0:T(8,128)S(1)} %get-tuple-element.10), custom_call_target="InvertDiagBlocksLowerTriangular" | custom-call | tf_op jit(solution)/shard_map/triangular_solve | solution.py:78
  220.6 1.9 fusion.30
  222.5 0.1 multiply_bitcast_fusion
  222.6 1.2 copy.45
  223.8 0.7 copy.42
  (34 shorter events, 0.7 us)
Async XLA Ops:
  7.2 135.7 %all-gather.2.cloned.1.call-start = ((), (), s32[]{:S(2)}) async-start(), calls=%async_computation | async-start | bytes 3145728 | tf_op jit(solution)/shard_map/all_gather | solution.py:72
  9.0 0.8 copy-start.3
  9.0 0.8 copy-start.4
  9.0 0.8 copy-start.2
  10.2 4.3 %collective-permute-start = (f32[32,1,128]{2,0,1:T(8,128)S(1)}, f32[32,1,128]{2,0,1:T(8,128)S(1)}, u32[]{:S(2)}, u32[]{:S(2)}) collective-permute-start(f32[32,1,128]{2,0,1:T(8,128)S(1)} %get-tuple-element.35), channel_id=1, source_target_pairs={{4,0},{8,4},{12,8},{5,1},{9,5},{13,9},{6,2},{10,6},{14,10},{7,3},{... | collective-permute-start | bytes 49160 | tf_op jit(solution)/shard_map/ppermute | solution.py:22
  11.5 3.9 %collective-permute-start.1 = (f32[32,1,128]{2,0,1:T(8,128)S(1)}, f32[32,1,128]{2,0,1:T(8,128)S(1)}, u32[]{:S(2)}, u32[]{:S(2)}) collective-permute-start(f32[32,1,128]{2,0,1:T(8,128)S(1)} %get-tuple-element.34), channel_id=1, source_target_pairs={{0,4},{4,8},{8,12},{1,5},{5,9},{9,13},{2,6},{6,10},{10,14},{3,7},{... | collective-permute-start | bytes 49160 | tf_op jit(solution)/shard_map/ppermute | solution.py:20
  19.0 8.7 %collective-permute-start.2 = (f32[32,66,1]{1,0,2:T(8,128)S(1)}, f32[32,66,1]{1,0,2:T(8,128)S(1)}, u32[]{:S(2)}, u32[]{:S(2)}) collective-permute-start(f32[32,66,1]{1,0,2:T(8,128)S(1)} %copy.23), channel_id=1, source_target_pairs={{1,0},{2,1},{3,2},{5,4},{6,5},{7,6},{9,8},{10,9},{11,10},{13,12},{... | collective-permute-start | bytes 25352 | tf_op jit(solution)/shard_map/ppermute | solution.py:22
  22.2 7.5 %collective-permute-start.3 = (f32[32,66,1]{1,0,2:T(8,128)S(1)}, f32[32,66,1]{1,0,2:T(8,128)S(1)}, u32[]{:S(2)}, u32[]{:S(2)}) collective-permute-start(f32[32,66,1]{1,0,2:T(8,128)S(1)} %copy.25), channel_id=1, source_target_pairs={{0,1},{1,2},{2,3},{4,5},{5,6},{6,7},{8,9},{9,10},{10,11},{12,13},{... | collective-permute-start | bytes 25352 | tf_op jit(solution)/shard_map/ppermute | solution.py:20
  35.5 4.9 %collective-permute-start.4 = (f32[32,1,128]{2,0,1:T(8,128)S(1)}, f32[32,1,128]{2,0,1:T(8,128)S(1)}, u32[]{:S(2)}, u32[]{:S(2)}) collective-permute-start(f32[32,1,128]{2,0,1:T(8,128)S(1)} %get-tuple-element.33), channel_id=1, source_target_pairs={{4,0},{8,4},{12,8},{5,1},{9,5},{13,9},{6,2},{10,6},{14,10},{7,3},{... | collective-permute-start | bytes 49160 | tf_op jit(solution)/shard_map/ppermute | solution.py:22
  36.8 4.4 %collective-permute-start.5 = (f32[32,1,128]{2,0,1:T(8,128)S(1)}, f32[32,1,128]{2,0,1:T(8,128)S(1)}, u32[]{:S(2)}, u32[]{:S(2)}) collective-permute-start(f32[32,1,128]{2,0,1:T(8,128)S(1)} %get-tuple-element.32), channel_id=1, source_target_pairs={{0,4},{4,8},{8,12},{1,5},{5,9},{9,13},{2,6},{6,10},{10,14},{3,7},{... | collective-permute-start | bytes 49160 | tf_op jit(solution)/shard_map/ppermute | solution.py:20
  44.5 6.6 %collective-permute-start.6 = (f32[32,66,1]{1,0,2:T(8,128)S(1)}, f32[32,66,1]{1,0,2:T(8,128)S(1)}, u32[]{:S(2)}, u32[]{:S(2)}) collective-permute-start(f32[32,66,1]{1,0,2:T(8,128)S(1)} %copy.27), channel_id=1, source_target_pairs={{1,0},{2,1},{3,2},{5,4},{6,5},{7,6},{9,8},{10,9},{11,10},{13,12},{... | collective-permute-start | bytes 25352 | tf_op jit(solution)/shard_map/ppermute | solution.py:22
  46.5 6.0 %collective-permute-start.7 = (f32[32,66,1]{1,0,2:T(8,128)S(1)}, f32[32,66,1]{1,0,2:T(8,128)S(1)}, u32[]{:S(2)}, u32[]{:S(2)}) collective-permute-start(f32[32,66,1]{1,0,2:T(8,128)S(1)} %copy.29), channel_id=1, source_target_pairs={{0,1},{1,2},{2,3},{4,5},{5,6},{6,7},{8,9},{9,10},{10,11},{12,13},{... | collective-permute-start | bytes 25352 | tf_op jit(solution)/shard_map/ppermute | solution.py:20
  57.8 5.9 %collective-permute-start.8 = (f32[32,1,128]{2,0,1:T(8,128)S(1)}, f32[32,1,128]{2,0,1:T(8,128)S(1)}, u32[]{:S(2)}, u32[]{:S(2)}) collective-permute-start(f32[32,1,128]{2,0,1:T(8,128)S(1)} %get-tuple-element.31), channel_id=1, source_target_pairs={{4,0},{8,4},{12,8},{5,1},{9,5},{13,9},{6,2},{10,6},{14,10},{7,3},{... | collective-permute-start | bytes 49160 | tf_op jit(solution)/shard_map/ppermute | solution.py:22
  59.1 5.4 %collective-permute-start.9 = (f32[32,1,128]{2,0,1:T(8,128)S(1)}, f32[32,1,128]{2,0,1:T(8,128)S(1)}, u32[]{:S(2)}, u32[]{:S(2)}) collective-permute-start(f32[32,1,128]{2,0,1:T(8,128)S(1)} %get-tuple-element.30), channel_id=1, source_target_pairs={{0,4},{4,8},{8,12},{1,5},{5,9},{9,13},{2,6},{6,10},{10,14},{3,7},{... | collective-permute-start | bytes 49160 | tf_op jit(solution)/shard_map/ppermute | solution.py:20
  65.7 6.7 %collective-permute-start.10 = (f32[32,66,1]{1,0,2:T(8,128)S(1)}, f32[32,66,1]{1,0,2:T(8,128)S(1)}, u32[]{:S(2)}, u32[]{:S(2)}) collective-permute-start(f32[32,66,1]{1,0,2:T(8,128)S(1)} %copy.31), channel_id=1, source_target_pairs={{1,0},{2,1},{3,2},{5,4},{6,5},{7,6},{9,8},{10,9},{11,10},{13,12},{... | collective-permute-start | bytes 25352 | tf_op jit(solution)/shard_map/ppermute | solution.py:22
  67.7 6.0 %collective-permute-start.11 = (f32[32,66,1]{1,0,2:T(8,128)S(1)}, f32[32,66,1]{1,0,2:T(8,128)S(1)}, u32[]{:S(2)}, u32[]{:S(2)}) collective-permute-start(f32[32,66,1]{1,0,2:T(8,128)S(1)} %copy.33), channel_id=1, source_target_pairs={{0,1},{1,2},{2,3},{4,5},{5,6},{6,7},{8,9},{9,10},{10,11},{12,13},{... | collective-permute-start | bytes 25352 | tf_op jit(solution)/shard_map/ppermute | solution.py:20
  79.0 6.8 %collective-permute-start.12 = (f32[32,1,128]{2,0,1:T(8,128)S(1)}, f32[32,1,128]{2,0,1:T(8,128)S(1)}, u32[]{:S(2)}, u32[]{:S(2)}) collective-permute-start(f32[32,1,128]{2,0,1:T(8,128)S(1)} %get-tuple-element.29), channel_id=1, source_target_pairs={{4,0},{8,4},{12,8},{5,1},{9,5},{13,9},{6,2},{10,6},{14,10},{7,3},{... | collective-permute-start | bytes 49160 | tf_op jit(solution)/shard_map/ppermute | solution.py:22
  80.3 6.4 %collective-permute-start.13 = (f32[32,1,128]{2,0,1:T(8,128)S(1)}, f32[32,1,128]{2,0,1:T(8,128)S(1)}, u32[]{:S(2)}, u32[]{:S(2)}) collective-permute-start(f32[32,1,128]{2,0,1:T(8,128)S(1)} %get-tuple-element.28), channel_id=1, source_target_pairs={{0,4},{4,8},{8,12},{1,5},{5,9},{9,13},{2,6},{6,10},{10,14},{3,7},{... | collective-permute-start | bytes 49160 | tf_op jit(solution)/shard_map/ppermute | solution.py:20
  89.9 6.7 %collective-permute-start.14 = (f32[32,66,1]{1,0,2:T(8,128)S(1)}, f32[32,66,1]{1,0,2:T(8,128)S(1)}, u32[]{:S(2)}, u32[]{:S(2)}) collective-permute-start(f32[32,66,1]{1,0,2:T(8,128)S(1)} %copy.35), channel_id=1, source_target_pairs={{1,0},{2,1},{3,2},{5,4},{6,5},{7,6},{9,8},{10,9},{11,10},{13,12},{... | collective-permute-start | bytes 25352 | tf_op jit(solution)/shard_map/ppermute | solution.py:22
  91.9 8.0 %copy-start.1 = (f32[32,64,128]{2,0,1:T(8,128)S(1)}, f32[32,64,128]{2,0,1:T(8,128)}, u32[]{:S(2)}) copy-start(f32[32,64,128]{2,0,1:T(8,128)} %get-tuple-element.13) | copy-start | bytes 3145732
  91.9 6.1 %collective-permute-start.15 = (f32[32,66,1]{1,0,2:T(8,128)S(1)}, f32[32,66,1]{1,0,2:T(8,128)S(1)}, u32[]{:S(2)}, u32[]{:S(2)}) collective-permute-start(f32[32,66,1]{1,0,2:T(8,128)S(1)} %copy.37), channel_id=1, source_target_pairs={{0,1},{1,2},{2,3},{4,5},{5,6},{6,7},{8,9},{9,10},{10,11},{12,13},{... | collective-permute-start | bytes 25352 | tf_op jit(solution)/shard_map/ppermute | solution.py:20
  142.9 77.7 %copy-start = (f32[64,8192]{1,0:T(8,128)S(1)}, f32[64,8192]{1,0:T(8,128)}, u32[]{:S(2)}) copy-start(f32[64,8192]{1,0:T(8,128)} %all-gather.2.cloned.1.call-done) | copy-start | bytes 6291460
Sparse Core Ops, SparseCore 0:
  103.2 39.6 all-gather.1
where the time goes:
time: 232 us; the launch traced here: 231 us
  blocking collectives  61.3 us (26%)
  starting transfers between devices  46.5 us (20%)
  waiting for transfers between devices  43.9 us (19%)
  local copies, waits for them, and re-layouts  30.7 us (13%)
  other arithmetic  28.4 us (12%)
  between operations  14.4 us (6%)
  matrix products  6.09 us (3%)
    psum x1, blocking collectives, shards(): gram_matrix = lax.psum(local_gram, ('sx', 'sy'))  61.3 us
    all_gather x1, waiting for transfers between devices, shards(): all_rows = lax.all_gather(response, 'dir', axis=0, tiled=True)  39.8 us
    ppermute x8, starting transfers between devices, with_halo(): lax.ppermute(tail, axis, [(i, (i + 1) % count) for i in range(ends)])  36.2 us
    slice x8, local copies, waits for them, and re-layouts, with_halo(): head = lax.slice_in_dim(cells, 0, width, axis=dim)  11.2 us
    mul x4, other arithmetic, apply_step(): weighted = stiffness * wavefield  11 us
    ppermute x8, starting transfers between devices, with_halo(): lax.ppermute(head, axis, [((i + 1) % count, i) for i in range(ends)])  10.3 us
    ppermute x4, local copies, waits for them, and re-layouts, with_halo(): lax.ppermute(tail, axis, [(i, (i + 1) % count) for i in range(ends)])  7.68 us
    another operation x3, other arithmetic, shards(): factor_low = jnp.linalg.cholesky(gram_matrix)  6.52 us
  transfers between devices with their start and end apart: 17, of which 8 were waited for; matrix products, arithmetic and copies ran while one was open for 4% of the time, Pallas kernels for 0%

commit v1 on v0

--- a/solution.py
+++ b/solution.py
@@ -73,7 +73,7 @@
     local_gram = jnp.dot(
         all_rows, all_rows.T, precision=lax.Precision.HIGHEST, preferred_element_type=jnp.float32
     )
-    gram_matrix = lax.psum(local_gram, ("sx", "sy"))
+    gram_matrix = jnp.sum(lax.all_gather(local_gram, ("sx", "sy")), axis=0)
     factor_low = jnp.linalg.cholesky(gram_matrix)
     orthonormal = lax.linalg.triangular_solve(factor_low, all_rows, left_side=True, lower=True)
     factor_r = factor_low.T

time: 232 us -> 208 us (0.90)
  blocking collectives: 61.3 us -> 37.1 us
    psum x1 -> x0, blocking collectives: 61.3 us -> none  [shards(): gram_matrix = lax.psum(local_gram, ('sx', 'sy'))]
    all_gather x0 -> x1, blocking collectives: none -> 37.1 us  [shards(): gram_matrix = jnp.sum(lax.all_gather(local_gram, ('sx', 'sy')), axis=0)]
where the time goes in v1:
time: 208 us; the launch traced here: 207 us
  starting transfers between devices  46.5 us (22%)
  waiting for transfers between devices  43.9 us (21%)
  blocking collectives  37.1 us (18%)
  local copies, waits for them, and re-layouts  30.7 us (15%)
  other arithmetic  28.5 us (14%)
  between operations  14.4 us (7%)
  matrix products  6.08 us (3%)
    all_gather x1, waiting for transfers between devices, shards(): all_rows = lax.all_gather(response, 'dir', axis=0, tiled=True)  39.8 us
    all_gather x1, blocking collectives, shards(): gram_matrix = jnp.sum(lax.all_gather(local_gram, ('sx', 'sy')), axis=0)  37.1 us
    ppermute x8, starting transfers between devices, with_halo(): lax.ppermute(tail, axis, [(i, (i + 1) % count) for i in range(ends)])  36.2 us
    slice x8, local copies, waits for them, and re-layouts, with_halo(): head = lax.slice_in_dim(cells, 0, width, axis=dim)  11.2 us
    mul x4, other arithmetic, apply_step(): weighted = stiffness * wavefield  11 us
    ppermute x8, starting transfers between devices, with_halo(): lax.ppermute(head, axis, [((i + 1) % count, i) for i in range(ends)])  10.3 us
    ppermute x4, local copies, waits for them, and re-layouts, with_halo(): lax.ppermute(tail, axis, [(i, (i + 1) % count) for i in range(ends)])  7.68 us
    another operation x3, other arithmetic, shards(): factor_low = jnp.linalg.cholesky(gram_matrix)  6.52 us
  transfers between devices with their start and end apart: 17, of which 8 were waited for; matrix products, arithmetic and copies ran while one was open for 4% of the time, Pallas kernels for 0%

profile of v1, /device:TPU:0, one launch (start us, length us, event | category | flops | bytes accessed | tf_op | source)
XLA Modules:
  0.0 207.1 jit_solution(2844370236228669173)
XLA Ops:
  7.2 0.7 add_convert_fusion
  7.9 0.7 add_convert_fusion.1
  8.6 0.3 broadcast_multiply_fusion.3
  9.0 0.1 slice.164
  9.2 0.5 copy-done.3
  9.8 0.4 fusion.29
  10.2 1.3 collective-permute-start
  11.5 3.0 %collective-permute-start.1 = (f32[32,1,128]{2,0,1:T(8,128)S(1)}, f32[32,1,128]{2,0,1:T(8,128)S(1)}, u32[]{:S(2)}, u32[]{:S(2)}) collective-permute-start(f32[32,1,128]{2,0,1:T(8,128)S(1)} %get-tuple-element.34), channel_id=1, source_target_pairs={{0,4},{4,8},{8,12},{1,5},{5,9},{9,13},{2,6},{6,10},{10,14},{3,7},{... | collective-permute-start | bytes 49160 | tf_op jit(solution)/shard_map/ppermute | solution.py:20
  14.5 0.8 collective-permute-done.1
  15.4 1.8 fusion.39
  17.1 1.9 copy.20
  19.0 1.3 collective-permute-start.2
  20.3 1.9 copy.22
  22.2 5.6 %collective-permute-start.3 = (f32[32,66,1]{1,0,2:T(8,128)S(1)}, f32[32,66,1]{1,0,2:T(8,128)S(1)}, u32[]{:S(2)}, u32[]{:S(2)}) collective-permute-start(f32[32,66,1]{1,0,2:T(8,128)S(1)} %copy.22), channel_id=1, source_target_pairs={{0,1},{1,2},{2,3},{4,5},{5,6},{6,7},{8,9},{9,10},{10,11},{12,13},{... | collective-permute-start | bytes 25352 | tf_op jit(solution)/shard_map/ppermute | solution.py:20
  27.7 1.9 copy.21
  29.6 1.9 copy.23
  31.6 3.9 %broadcast_multiply_fusion.2 = (f32[32,64,128]{2,0,1:T(8,128)S(1)}, f32[32,64,128]{2,0,1:T(8,128)}) fusion(f32[64,128]{1,0:T(8,128)S(1)} %get-tuple-element.19, f32[32,64,128]{2,0,1:T(8,128)S(1)} %fusion.29, f32[32,1,128]{2,0,1:T(8,128)S(1)} %collective-permute-done, f32[32,1,128]{2,0,1:T(8,128)S(1)} %collective-permute-done.1, f32[32,66,1]{2,0,1:T(8,128)} %copy.23, ...), kind=kLoop, calls=%fused_computation.71 | loop fusion | flops 5505024 | bytes 4366848 | tf_op jit(solution)/shard_map/mul | solution.py:37
  35.5 1.3 collective-permute-start.4
  36.8 3.6 %collective-permute-start.5 = (f32[32,1,128]{2,0,1:T(8,128)S(1)}, f32[32,1,128]{2,0,1:T(8,128)S(1)}, u32[]{:S(2)}, u32[]{:S(2)}) collective-permute-start(f32[32,1,128]{2,0,1:T(8,128)S(1)} %get-tuple-element.32), channel_id=1, source_target_pairs={{0,4},{4,8},{8,12},{1,5},{5,9},{9,13},{2,6},{6,10},{10,14},{3,7},{... | collective-permute-start | bytes 49160 | tf_op jit(solution)/shard_map/ppermute | solution.py:20
  40.3 0.8 collective-permute-done.5
  41.2 1.4 fusion.38
  42.6 1.9 copy.24
  44.5 1.3 collective-permute-start.6
  45.8 0.7 copy.26
  46.5 4.5 %collective-permute-start.7 = (f32[32,66,1]{1,0,2:T(8,128)S(1)}, f32[32,66,1]{1,0,2:T(8,128)S(1)}, u32[]{:S(2)}, u32[]{:S(2)}) collective-permute-start(f32[32,66,1]{1,0,2:T(8,128)S(1)} %copy.26), channel_id=1, source_target_pairs={{0,1},{1,2},{2,3},{4,5},{5,6},{6,7},{8,9},{9,10},{10,11},{12,13},{... | collective-permute-start | bytes 25352 | tf_op jit(solution)/shard_map/ppermute | solution.py:20
  51.0 1.1 copy.25
  52.1 0.3 collective-permute-done.7
  52.5 1.9 copy.27
  54.4 3.4 %broadcast_multiply_fusion.1 = (f32[32,64,128]{2,0,1:T(8,128)S(1)}, f32[32,64,128]{2,0,1:T(8,128)}) fusion(f32[64,128]{1,0:T(8,128)S(1)} %get-tuple-element.19, f32[32,64,128]{2,0,1:T(8,128)} %get-tuple-element.17, f32[32,64,128]{2,0,1:T(8,128)S(1)} %get-tuple-element.16, f32[32,1,128]{2,0,1:T(8,128)S(1)} %collective-permute-done.4, ...), kind=kLoop, calls=%fused_computation.70 | loop fusion | flops 4194304 | bytes 4309504 | tf_op jit(solution)/shard_map/mul | solution.py:37
  57.8 1.3 collective-permute-start.8
  59.1 4.6 %collective-permute-start.9 = (f32[32,1,128]{2,0,1:T(8,128)S(1)}, f32[32,1,128]{2,0,1:T(8,128)S(1)}, u32[]{:S(2)}, u32[]{:S(2)}) collective-permute-start(f32[32,1,128]{2,0,1:T(8,128)S(1)} %get-tuple-element.30), channel_id=1, source_target_pairs={{0,4},{4,8},{8,12},{1,5},{5,9},{9,13},{2,6},{6,10},{10,14},{3,7},{... | collective-permute-start | bytes 49160 | tf_op jit(solution)/shard_map/ppermute | solution.py:20
  63.7 0.8 collective-permute-done.9
  64.6 0.4 fusion.37
  64.9 0.7 copy.28
  65.7 1.3 collective-permute-start.10
  67.0 0.7 copy.30
  67.7 4.7 %collective-permute-start.11 = (f32[32,66,1]{1,0,2:T(8,128)S(1)}, f32[32,66,1]{1,0,2:T(8,128)S(1)}, u32[]{:S(2)}, u32[]{:S(2)}) collective-permute-start(f32[32,66,1]{1,0,2:T(8,128)S(1)} %copy.30), channel_id=1, source_target_pairs={{0,1},{1,2},{2,3},{4,5},{5,6},{6,7},{8,9},{9,10},{10,11},{12,13},{... | collective-permute-start | bytes 25352 | tf_op jit(solution)/shard_map/ppermute | solution.py:20
  72.4 1.1 copy.29
  73.5 0.2 collective-permute-done.11
  73.7 1.9 copy.31
  75.6 3.4 %broadcast_multiply_fusion = (f32[32,64,128]{2,0,1:T(8,128)S(1)}, f32[32,64,128]{2,0,1:T(8,128)}) fusion(f32[64,128]{1,0:T(8,128)S(1)} %get-tuple-element.19, f32[32,64,128]{2,0,1:T(8,128)} %get-tuple-element.15, f32[32,64,128]{2,0,1:T(8,128)S(1)} %get-tuple-element.14, f32[32,1,128]{2,0,1:T(8,128)S(1)} %collective-permute-done.8, ...), kind=kLoop, calls=%fused_computation.69 | loop fusion | flops 4194304 | bytes 4309504 | tf_op jit(solution)/shard_map/mul | solution.py:37
  79.0 1.3 collective-permute-start.12
  80.3 5.5 %collective-permute-start.13 = (f32[32,1,128]{2,0,1:T(8,128)S(1)}, f32[32,1,128]{2,0,1:T(8,128)S(1)}, u32[]{:S(2)}, u32[]{:S(2)}) collective-permute-start(f32[32,1,128]{2,0,1:T(8,128)S(1)} %get-tuple-element.28), channel_id=1, source_target_pairs={{0,4},{4,8},{8,12},{1,5},{5,9},{9,13},{2,6},{6,10},{10,14},{3,7},{... | collective-permute-start | bytes 49160 | tf_op jit(solution)/shard_map/ppermute | solution.py:20
  85.8 0.8 collective-permute-done.13
  86.7 1.4 fusion.36
  88.1 1.9 copy.32
  89.9 1.3 collective-permute-start.14
  91.2 0.7 copy.34
  91.9 4.7 %collective-permute-start.15 = (f32[32,66,1]{1,0,2:T(8,128)S(1)}, f32[32,66,1]{1,0,2:T(8,128)S(1)}, u32[]{:S(2)}, u32[]{:S(2)}) collective-permute-start(f32[32,66,1]{1,0,2:T(8,128)S(1)} %copy.34), channel_id=1, source_target_pairs={{0,1},{1,2},{2,3},{4,5},{5,6},{6,7},{8,9},{9,10},{10,11},{12,13},{... | collective-permute-start | bytes 25352 | tf_op jit(solution)/shard_map/ppermute | solution.py:20
  96.6 1.1 copy.33
  97.7 0.3 collective-permute-done.15
  98.1 1.9 copy.35
  100.0 3.1 %copy_bitcast_fusion = f32[32,8192]{1,0:T(8,128)} fusion(f32[32,64,128]{2,0,1:T(8,128)S(1)} %copy-done.1, f32[32,66,1]{2,0,1:T(8,128)} %copy.35, f32[32,1,128]{2,0,1:T(8,128)S(1)} %collective-permute-done.12, f32[32,64,128]{2,0,1:T(8,128)S(1)} %get-tuple-element.12, f32[32,1,128]{2,0,1:T(8,128)S(1)} %collective-permute-done.13, f32[32,66,1]{2,0,1:T(8,128)S(1)} %copy.33, ...), kind=kLoop, calls=%fused_computation.4 | loop fusion | flops 4194304 | bytes 3260928 | tf_op jit(solution)/shard_map/reshape | solution.py:64
  103.1 39.8 %all-gather.3.cloned.1.call-done = f32[64,8192]{1,0:T(8,128)} async-done(((f32[32,8192]{1,0:T(8,128)}), f32[64,8192]{1,0:T(8,128)}) %all-gather.3.cloned.1.call-update) | async-done | bytes 2097168 | tf_op jit(solution)/shard_map/all_gather | solution.py:72
  142.9 4.2 %fusion.44 = f32[64,64]{1,0:T(8,128)S(1)} fusion(f32[64,8192]{1,0:T(8,128)} %all-gather.3.cloned.1.call-done), kind=kOutput, calls=%fused_computation.96 | convolution fusion | flops 402653184 | bytes 2113536 | tf_op jit(solution)/shard_map/dot_general | solution.py:73
  147.0 37.1 %all-gather = f32[1024,64]{1,0:T(8,128)S(1)} all-gather(f32[64,64]{1,0:T(8,128)S(1)} %fusion.44), channel_id=2, replica_groups=mesh['dir'=2,'sx'=4,'sy'=4] {'sx','sy'}, dimensions={0}, use_global_device_ids=true | all-gather | bytes 278528 | tf_op jit(solution)/shard_map/all_gather | solution.py:76
  184.2 5.8 %cholesky.16 = f32[64,64]{1,0:T(8,128)S(1)} custom-call(f32[64,64]{1,0:T(8,128)S(1)} %fusion.32), custom_call_target="Cholesky" | custom-call | tf_op jit(solution)/shard_map/jit(cholesky)/cholesky | solution.py:77
  190.1 0.6 compare_reduce_fusion
  190.8 0.7 select_bitcast_fusion
  191.4 4.9 %custom-call.6 = f32[1,64,64]{1,2,0:T(8,128)S(1)} custom-call(f32[1,64,64]{2,1,0:T(8,128)S(1)} %get-tuple-element.10), custom_call_target="InvertDiagBlocksLowerTriangular" | custom-call | tf_op jit(solution)/shard_map/triangular_solve | solution.py:78
  196.4 1.9 fusion.30
  198.3 0.1 multiply_bitcast_fusion
  198.4 1.2 copy.40
  199.6 0.7 copy.38
  (35 shorter events, 0.7 us)
Async XLA Ops:
  7.2 135.7 %all-gather.3.cloned.1.call-start = ((), (), s32[]{:S(2)}) async-start(), calls=%async_computation | async-start | bytes 3145728 | tf_op jit(solution)/shard_map/all_gather | solution.py:72
  9.0 0.8 copy-start.3
  9.0 0.8 copy-start.4
  9.0 0.8 copy-start.2
  10.2 4.3 %collective-permute-start = (f32[32,1,128]{2,0,1:T(8,128)S(1)}, f32[32,1,128]{2,0,1:T(8,128)S(1)}, u32[]{:S(2)}, u32[]{:S(2)}) collective-permute-start(f32[32,1,128]{2,0,1:T(8,128)S(1)} %get-tuple-element.35), channel_id=1, source_target_pairs={{4,0},{8,4},{12,8},{5,1},{9,5},{13,9},{6,2},{10,6},{14,10},{7,3},{... | collective-permute-start | bytes 49160 | tf_op jit(solution)/shard_map/ppermute | solution.py:22
  11.5 3.9 %collective-permute-start.1 = (f32[32,1,128]{2,0,1:T(8,128)S(1)}, f32[32,1,128]{2,0,1:T(8,128)S(1)}, u32[]{:S(2)}, u32[]{:S(2)}) collective-permute-start(f32[32,1,128]{2,0,1:T(8,128)S(1)} %get-tuple-element.34), channel_id=1, source_target_pairs={{0,4},{4,8},{8,12},{1,5},{5,9},{9,13},{2,6},{6,10},{10,14},{3,7},{... | collective-permute-start | bytes 49160 | tf_op jit(solution)/shard_map/ppermute | solution.py:20
  19.0 8.7 %collective-permute-start.2 = (f32[32,66,1]{1,0,2:T(8,128)S(1)}, f32[32,66,1]{1,0,2:T(8,128)S(1)}, u32[]{:S(2)}, u32[]{:S(2)}) collective-permute-start(f32[32,66,1]{1,0,2:T(8,128)S(1)} %copy.20), channel_id=1, source_target_pairs={{1,0},{2,1},{3,2},{5,4},{6,5},{7,6},{9,8},{10,9},{11,10},{13,12},{... | collective-permute-start | bytes 25352 | tf_op jit(solution)/shard_map/ppermute | solution.py:22
  22.2 7.5 %collective-permute-start.3 = (f32[32,66,1]{1,0,2:T(8,128)S(1)}, f32[32,66,1]{1,0,2:T(8,128)S(1)}, u32[]{:S(2)}, u32[]{:S(2)}) collective-permute-start(f32[32,66,1]{1,0,2:T(8,128)S(1)} %copy.22), channel_id=1, source_target_pairs={{0,1},{1,2},{2,3},{4,5},{5,6},{6,7},{8,9},{9,10},{10,11},{12,13},{... | collective-permute-start | bytes 25352 | tf_op jit(solution)/shard_map/ppermute | solution.py:20
  35.5 4.9 %collective-permute-start.4 = (f32[32,1,128]{2,0,1:T(8,128)S(1)}, f32[32,1,128]{2,0,1:T(8,128)S(1)}, u32[]{:S(2)}, u32[]{:S(2)}) collective-permute-start(f32[32,1,128]{2,0,1:T(8,128)S(1)} %get-tuple-element.33), channel_id=1, source_target_pairs={{4,0},{8,4},{12,8},{5,1},{9,5},{13,9},{6,2},{10,6},{14,10},{7,3},{... | collective-permute-start | bytes 49160 | tf_op jit(solution)/shard_map/ppermute | solution.py:22
  36.8 4.4 %collective-permute-start.5 = (f32[32,1,128]{2,0,1:T(8,128)S(1)}, f32[32,1,128]{2,0,1:T(8,128)S(1)}, u32[]{:S(2)}, u32[]{:S(2)}) collective-permute-start(f32[32,1,128]{2,0,1:T(8,128)S(1)} %get-tuple-element.32), channel_id=1, source_target_pairs={{0,4},{4,8},{8,12},{1,5},{5,9},{9,13},{2,6},{6,10},{10,14},{3,7},{... | collective-permute-start | bytes 49160 | tf_op jit(solution)/shard_map/ppermute | solution.py:20
  44.5 6.6 %collective-permute-start.6 = (f32[32,66,1]{1,0,2:T(8,128)S(1)}, f32[32,66,1]{1,0,2:T(8,128)S(1)}, u32[]{:S(2)}, u32[]{:S(2)}) collective-permute-start(f32[32,66,1]{1,0,2:T(8,128)S(1)} %copy.24), channel_id=1, source_target_pairs={{1,0},{2,1},{3,2},{5,4},{6,5},{7,6},{9,8},{10,9},{11,10},{13,12},{... | collective-permute-start | bytes 25352 | tf_op jit(solution)/shard_map/ppermute | solution.py:22
  46.5 6.0 %collective-permute-start.7 = (f32[32,66,1]{1,0,2:T(8,128)S(1)}, f32[32,66,1]{1,0,2:T(8,128)S(1)}, u32[]{:S(2)}, u32[]{:S(2)}) collective-permute-start(f32[32,66,1]{1,0,2:T(8,128)S(1)} %copy.26), channel_id=1, source_target_pairs={{0,1},{1,2},{2,3},{4,5},{5,6},{6,7},{8,9},{9,10},{10,11},{12,13},{... | collective-permute-start | bytes 25352 | tf_op jit(solution)/shard_map/ppermute | solution.py:20
  57.8 5.9 %collective-permute-start.8 = (f32[32,1,128]{2,0,1:T(8,128)S(1)}, f32[32,1,128]{2,0,1:T(8,128)S(1)}, u32[]{:S(2)}, u32[]{:S(2)}) collective-permute-start(f32[32,1,128]{2,0,1:T(8,128)S(1)} %get-tuple-element.31), channel_id=1, source_target_pairs={{4,0},{8,4},{12,8},{5,1},{9,5},{13,9},{6,2},{10,6},{14,10},{7,3},{... | collective-permute-start | bytes 49160 | tf_op jit(solution)/shard_map/ppermute | solution.py:22
  59.1 5.4 %collective-permute-start.9 = (f32[32,1,128]{2,0,1:T(8,128)S(1)}, f32[32,1,128]{2,0,1:T(8,128)S(1)}, u32[]{:S(2)}, u32[]{:S(2)}) collective-permute-start(f32[32,1,128]{2,0,1:T(8,128)S(1)} %get-tuple-element.30), channel_id=1, source_target_pairs={{0,4},{4,8},{8,12},{1,5},{5,9},{9,13},{2,6},{6,10},{10,14},{3,7},{... | collective-permute-start | bytes 49160 | tf_op jit(solution)/shard_map/ppermute | solution.py:20
  65.7 6.7 %collective-permute-start.10 = (f32[32,66,1]{1,0,2:T(8,128)S(1)}, f32[32,66,1]{1,0,2:T(8,128)S(1)}, u32[]{:S(2)}, u32[]{:S(2)}) collective-permute-start(f32[32,66,1]{1,0,2:T(8,128)S(1)} %copy.28), channel_id=1, source_target_pairs={{1,0},{2,1},{3,2},{5,4},{6,5},{7,6},{9,8},{10,9},{11,10},{13,12},{... | collective-permute-start | bytes 25352 | tf_op jit(solution)/shard_map/ppermute | solution.py:22
  67.7 6.0 %collective-permute-start.11 = (f32[32,66,1]{1,0,2:T(8,128)S(1)}, f32[32,66,1]{1,0,2:T(8,128)S(1)}, u32[]{:S(2)}, u32[]{:S(2)}) collective-permute-start(f32[32,66,1]{1,0,2:T(8,128)S(1)} %copy.30), channel_id=1, source_target_pairs={{0,1},{1,2},{2,3},{4,5},{5,6},{6,7},{8,9},{9,10},{10,11},{12,13},{... | collective-permute-start | bytes 25352 | tf_op jit(solution)/shard_map/ppermute | solution.py:20
  79.0 6.8 %collective-permute-start.12 = (f32[32,1,128]{2,0,1:T(8,128)S(1)}, f32[32,1,128]{2,0,1:T(8,128)S(1)}, u32[]{:S(2)}, u32[]{:S(2)}) collective-permute-start(f32[32,1,128]{2,0,1:T(8,128)S(1)} %get-tuple-element.29), channel_id=1, source_target_pairs={{4,0},{8,4},{12,8},{5,1},{9,5},{13,9},{6,2},{10,6},{14,10},{7,3},{... | collective-permute-start | bytes 49160 | tf_op jit(solution)/shard_map/ppermute | solution.py:22
  80.3 6.4 %collective-permute-start.13 = (f32[32,1,128]{2,0,1:T(8,128)S(1)}, f32[32,1,128]{2,0,1:T(8,128)S(1)}, u32[]{:S(2)}, u32[]{:S(2)}) collective-permute-start(f32[32,1,128]{2,0,1:T(8,128)S(1)} %get-tuple-element.28), channel_id=1, source_target_pairs={{0,4},{4,8},{8,12},{1,5},{5,9},{9,13},{2,6},{6,10},{10,14},{3,7},{... | collective-permute-start | bytes 49160 | tf_op jit(solution)/shard_map/ppermute | solution.py:20
  89.9 6.7 %collective-permute-start.14 = (f32[32,66,1]{1,0,2:T(8,128)S(1)}, f32[32,66,1]{1,0,2:T(8,128)S(1)}, u32[]{:S(2)}, u32[]{:S(2)}) collective-permute-start(f32[32,66,1]{1,0,2:T(8,128)S(1)} %copy.32), channel_id=1, source_target_pairs={{1,0},{2,1},{3,2},{5,4},{6,5},{7,6},{9,8},{10,9},{11,10},{13,12},{... | collective-permute-start | bytes 25352 | tf_op jit(solution)/shard_map/ppermute | solution.py:22
  91.9 8.0 %copy-start.1 = (f32[32,64,128]{2,0,1:T(8,128)S(1)}, f32[32,64,128]{2,0,1:T(8,128)}, u32[]{:S(2)}) copy-start(f32[32,64,128]{2,0,1:T(8,128)} %get-tuple-element.13) | copy-start | bytes 3145732
  91.9 6.1 %collective-permute-start.15 = (f32[32,66,1]{1,0,2:T(8,128)S(1)}, f32[32,66,1]{1,0,2:T(8,128)S(1)}, u32[]{:S(2)}, u32[]{:S(2)}) collective-permute-start(f32[32,66,1]{1,0,2:T(8,128)S(1)} %copy.34), channel_id=1, source_target_pairs={{0,1},{1,2},{2,3},{4,5},{5,6},{6,7},{8,9},{9,10},{10,11},{12,13},{... | collective-permute-start | bytes 25352 | tf_op jit(solution)/shard_map/ppermute | solution.py:20
  142.9 53.5 %copy-start = (f32[64,8192]{1,0:T(8,128)S(1)}, f32[64,8192]{1,0:T(8,128)}, u32[]{:S(2)}) copy-start(f32[64,8192]{1,0:T(8,128)} %all-gather.3.cloned.1.call-done) | copy-start | bytes 6291460
Sparse Core Ops, SparseCore 0:
  103.2 39.6 all-gather.2
